TPU v7x, 256 devices: a whole 4x4x8 slice. The times are simulated.
256 devices in a mesh: rep: 16 (over y_lo, z), tp: 16 (over x, y_hi, core).
Axes of the slice: x: 4, y: 4 (y_hi: 2, y_lo: 2; y = y_hi * 2 + y_lo), z: 8, core: 2. Of those that a mesh axis runs over, the one named last changes fastest.
Arguments:
- tokens: bfloat16 [16384, 8192], P('rep', 'tp'), may hold values from -6 to 6
- grad_out: bfloat16 [16384, 4096], P('rep', 'tp'), may hold values from -0.046875 to 0.046875
- lengths: int32 [16, 16], replicated, may hold values from 0 to 256, as said below
- master: float32 [8192, 2048], P('rep', 'tp'), may hold values from -3 to 3
- first: float32 [8192, 2048], P('rep', 'tp'), may hold values from -6 to 6
- second: float32 [8192, 2048], P('rep', 'tp'), may hold values from 0.25 to 4
Outputs:
- new_master: float32 [8192, 2048], P('rep', 'tp')
- new_first: float32 [8192, 2048], P('rep', 'tp')
- new_second: float32 [8192, 2048], P('rep', 'tp')
- healthy_weights: bfloat16 [8192, 2048], P(None, 'tp')
- slot_weights: bfloat16 [16, 8192, 4096], P('rep', None, 'tp')
Inputs may be any that keep to these rules, and one draw needn't show every extreme that they name: `lengths`: each row is one replica's split of the 2048 columns over its devices in tp order: the entries are multiples of 64, sum to 2048, the nonzero ones come first and number at least half of the row; a row is either all 128 or has an entry equal to 256, and some row has an entry equal to 256.
All inputs are finite; a program needn't handle non-finite values.
Results may differ from a plain program's by a relative error of at most 0.0019.
Values may be sent and summed in bfloat16 or wider, within the bound.
No kernel may reach another device: no remote copies, remote signals or barrier semaphores. Data moves between devices by JAX's collectives and lax.ppermute only.
A program may use at most 128 MiB of HBM per device.

v0:
```python
import jax
import jax.numpy as jnp
from jax import lax
from jax.sharding import Mesh
from jax.sharding import PartitionSpec as P

COLS = 2048
STEP = 1000
REP = ("rep_0", "rep_1")
decay_first = 0.9
decay_second = 0.999
learning_rate = 0.02
weight_decay = 0.1
epsilon = 1e-08


def own_block(parts, axes, turns):
    inside = parts.shape[1:]
    parts = parts.reshape(*(lax.axis_size(a) for a in axes), *inside)
    parts = jnp.moveaxis(parts, turns, range(len(axes))).reshape(-1, *inside)
    for k in turns:
        parts = lax.psum_scatter(parts, axes[k], scatter_dimension=0, tiled=True)
    return parts[0]


def in_blocks(value, dim, size):
    before, after = (value.shape[:dim], value.shape[dim + 1 :])
    return jnp.moveaxis(value.reshape(*before, size, -1, *after), dim, 0)


def summed_rows(value, axes, turns, dim):
    size = lax.axis_size(axes)
    return own_block(in_blocks(value, dim, size), axes, turns)


def from_everyone(value, axis):
    copies = jnp.broadcast_to(value, (lax.axis_size(axis), *value.shape))
    return lax.all_to_all(copies, axis, split_axis=0, concat_axis=0, tiled=True)


def laid_out(parts, dim):
    shape = list(parts.shape[1:])
    shape[dim] *= parts.shape[0]
    return jnp.moveaxis(parts, 0, dim).reshape(shape)


def gathered_copies(value, axis, dim):
    parts = from_everyone(value, axis)
    return laid_out(parts, dim)


def adam_update(master, first, second, gradient):
    scale_first = 1.0 - decay_first**STEP
    scale_second = 1.0 - decay_second**STEP
    new_first = decay_first * first + (1.0 - decay_first) * gradient
    new_second = decay_second * second + (1.0 - decay_second) * gradient * gradient
    direction = new_first / scale_first / (jnp.sqrt(new_second / scale_second) + epsilon)
    new_master = master - learning_rate * (direction + weight_decay * master)
    return (new_master, new_first, new_second)


def on_device(tokens, grad_out, lengths, master, first, second):
    shards = lax.axis_size("tp")
    replicas = lax.axis_size(REP)
    column_index = lax.axis_index("tp")
    replica_index = lax.axis_index(REP)
    token_count = tokens.shape[0]
    slot_width = grad_out.shape[1]
    block_width = COLS // shards
    begins_all = jnp.cumsum(lengths, axis=1) - lengths
    is_mine = jnp.arange(shards, dtype=jnp.int32) == column_index
    own_lengths = lax.dynamic_index_in_dim(lengths, replica_index, 0, keepdims=False)
    own_begins = lax.dynamic_index_in_dim(begins_all, replica_index, 0, keepdims=False)
    my_begin = jnp.sum(jnp.where(is_mine, own_begins, 0))
    my_length = jnp.sum(jnp.where(is_mine, own_lengths, 0))
    columns = jnp.arange(COLS, dtype=jnp.int32)
    offset = columns - my_begin
    inside = (offset >= 0) & (offset < my_length)
    picked = jnp.take(grad_out, jnp.clip(offset, 0, slot_width - 1), axis=1)
    spread = jnp.where(inside[None, :], picked, jnp.zeros_like(picked)).reshape(
        token_count, shards, block_width
    )
    received = lax.all_to_all(spread, "tp", split_axis=1, concat_axis=1, tiled=True)
    grad_block = jnp.sum(received, axis=1)
    grad_columns = lax.dot_general(
        lax.all_gather(tokens, "tp", axis=1, tiled=True),
        grad_block,
        (((0,), (0,)), ((), ())),
        preferred_element_type=jnp.float32,
    )
    summed = summed_rows(grad_columns.astype(jnp.bfloat16), REP, (1, 0), 0).astype(jnp.float32)
    new_master, new_first, new_second = adam_update(master, first, second, summed)
    weights = new_master.astype(jnp.bfloat16)
    healthy = gathered_copies(weights, REP, 0)
    replica_rows = lax.all_gather(weights, "tp", axis=1, tiled=True)
    slot_begins = jnp.sum(jnp.where(is_mine[None, :], begins_all, 0), axis=1)
    slot_lengths = jnp.sum(jnp.where(is_mine[None, :], lengths, 0), axis=1)
    within = jnp.arange(slot_width, dtype=jnp.int32)
    source_cols = slot_begins[:, None] + within[None, :]
    valid = within[None, :] < slot_lengths[:, None]
    taken = jnp.take(replica_rows, jnp.clip(source_cols, 0, COLS - 1).reshape(-1), axis=1)
    outgoing = jnp.where(valid.reshape(-1)[None, :], taken, jnp.zeros_like(taken))
    outgoing = outgoing.reshape(replica_rows.shape[0], replicas, slot_width)
    arrived = lax.all_to_all(outgoing, REP, split_axis=1, concat_axis=0, tiled=True)
    slot_weights = arrived.reshape(1, -1, slot_width)
    return (new_master, new_first, new_second, healthy, slot_weights)


def solution(mesh):
    torus = Mesh(mesh.devices.reshape(2, 8, mesh.shape["tp"]), ("rep_0", "rep_1", "tp"))
    placed = (P(REP, "tp"), P(REP, "tp"), P(), P(REP, "tp"), P(REP, "tp"), P(REP, "tp"))
    return jax.shard_map(
        on_device,
        mesh=torus,
        in_specs=placed,
        out_specs=(P(REP, "tp"), P(REP, "tp"), P(REP, "tp"), P(None, "tp"), P(REP, None, "tp")),
        check_vma=False,
    )
```

profile of v0, /device:TPU:32, one launch (start us, length us, event | category | flops | bytes accessed | tf_op | source)
XLA Modules:
  0.0 450.8 jit_solution(10688095374911271748)
XLA Ops:
  8.0 0.9 reduce_window_sum.11
  8.8 1.2 copy.34
  10.9 1.3 fusion.12
  12.9 9.6 %gather_fusion = bf16[2048,1024]{1,0:T(8,128)(2,1)} fusion(bf16[1024,256]{0,1:T(8,128)(2,1)S(1)} %copy.34, s32[2048]{0:T(1024)S(1)} %broadcast_clamp_fusion.1), kind=kCustom, calls=%fused_computation | custom fusion | bytes 8396800 | tf_op jit(solution)/shard_map/jit(_take)/gather | solution.py:79
  23.2 1.3 fusion.11
  24.5 3.1 select_select_fusion.1
  27.6 73.9 %all_to_all.25 = bf16[1024,16,128]{0,2,1:T(8,128)(2,1)} all-to-all(bf16[1024,16,128]{0,2,1:T(8,128)(2,1)S(1)} %select_select_fusion.1), channel_id=1, replica_groups=mesh['rep_0'=2,'rep_1'=8,'tp'=16] {'tp'}, dimensions={1} | all-to-all | bytes 8388608 | tf_op jit(solution)/shard_map/all_to_all | solution.py:83
  101.5 3.1 reduce_sum.50
  104.7 63.9 %all-gather.3.cloned.1.call-done = bf16[1024,8192]{1,0:T(8,128)(2,1)} async-done(((bf16[1024,512]{1,0:T(8,128)(2,1)}), bf16[1024,8192]{1,0:T(8,128)(2,1)}) %all-gather.3.cloned.1.call-update) | async-done | bytes 16777232 | tf_op jit(solution)/shard_map/all_gather | solution.py:86
  168.6 8.1 %convolution_convert_fusion = bf16[128,8192]{1,0:T(8,128)(2,1)S(1)} fusion(bf16[1024,128]{0,1:T(8,128)(2,1)S(1)} %reduce_sum.50, bf16[1024,8192]{1,0:T(8,128)(2,1)} %all-gather.3.cloned.1.call-done), kind=kOutput, calls=%fused_computation.2 | convolution fusion | flops 2148532224 | bytes 19136512 | tf_op jit(solution)/shard_map/dot_general | solution.py:85
  177.6 2.5 copy.35
  180.2 41.0 %reduce-scatter.3.cloned.1.call-done = bf16[2,512,128]{1,2,0:T(8,128)(2,1)} async-done(((bf16[16,512,128]{1,2,0:T(8,128)(2,1)}), bf16[2,512,128]{1,2,0:T(8,128)(2,1)}) %reduce-scatter.3.cloned.1.call-update) | async-done | bytes 262160 | tf_op jit(solution)/shard_map/reduce_scatter | solution.py:22
  221.7 18.0 %reduce-scatter.5.cloned.1.call-done = bf16[1,512,128]{1,2,0:T(8,128)(2,1)} async-done(((bf16[2,512,128]{1,2,0:T(8,128)(2,1)}), bf16[1,512,128]{1,2,0:T(8,128)(2,1)}) %reduce-scatter.5.cloned.1.call-update) | async-done | bytes 131088 | tf_op jit(solution)/shard_map/reduce_scatter | solution.py:22
  239.7 1.8 fusion.14
  241.5 1.0 copy.39
  242.5 1.7 broadcast_in_dim.78
  244.3 7.5 %all-to-all-start.1 = ((bf16[16,512,128]{2,1,0:T(8,128)(2,1)}), bf16[16,512,128]{2,1,0:T(8,128)(2,1)S(1)}, u32[]{:S(2)}, u32[]{:S(2)}) async-start(bf16[16,512,128]{2,1,0:T(8,128)(2,1)} %broadcast_in_dim.78), calls=%async_computation.3 | async-start | bytes 4194304 | tf_op jit(solution)/shard_map/all_to_all | solution.py:38
  252.0 52.9 %all-gather.5.cloned.1.call-done = bf16[512,2048]{0,1:T(8,128)(2,1)} async-done(((bf16[512,128]{0,1:T(8,128)(2,1)}), bf16[512,2048]{0,1:T(8,128)(2,1)}) %all-gather.5.cloned.1.call-update) | async-done | bytes 2097168 | tf_op jit(solution)/shard_map/all_gather | solution.py:95
  304.9 19.3 %gather_fusion.1 = bf16[4096,512]{1,0:T(8,128)(2,1)} fusion(bf16[512,2048]{0,1:T(8,128)(2,1)} %all-gather.5.cloned.1.call-done, s32[4096]{0:T(1024)S(1)} %broadcast_clamp_fusion), kind=kCustom, calls=%fused_computation.1 | custom fusion | bytes 8404992 | tf_op jit(solution)/shard_map/jit(_take)/gather | solution.py:101
  324.2 5.2 %select_select_fusion = bf16[512,16,256]{0,2,1:T(8,128)(2,1)} fusion(bf16[512,16,256]{0,2,1:T(8,128)(2,1)} %bitcast.43, pred[16,256]{1,0:T(8,128)(4,1)S(1)} %get-tuple-element.30, pred[16,256]{1,0:T(8,128)(4,1)S(1)} %get-tuple-element.29), kind=kLoop, calls=%fused_computation.3 | loop fusion | flops 4194304 | bytes 8396800 | tf_op jit(solution)/shard_map/jit(_where)/select_n | solution.py:102
  329.5 11.3 %all-to-all-start.2 = ((bf16[512,16,256]{0,2,1:T(8,128)(2,1)}), bf16[512,16,256]{0,2,1:T(8,128)(2,1)}, u32[]{:S(2)}, u32[]{:S(2)}) async-start(bf16[512,16,256]{0,2,1:T(8,128)(2,1)} %select_select_fusion), calls=%async_computation.4 | async-start | bytes 8388608 | tf_op jit(solution)/shard_map/all_to_all | solution.py:104
  343.2 93.3 %all-to-all-done.2 = bf16[512,16,256]{0,2,1:T(8,128)(2,1)} async-done(((bf16[512,16,256]{0,2,1:T(8,128)(2,1)}), bf16[512,16,256]{0,2,1:T(8,128)(2,1)}, u32[]{:S(2)}, u32[]{:S(2)}) %all-to-all-start.2) | async-done | bytes 4194336 | tf_op jit(solution)/shard_map/all_to_all | solution.py:104
  436.6 6.4 %copy.40 = bf16[16,512,1,256]{3,1,0,2:T(8,128)(2,1)} copy(bf16[16,512,1,256]{1,3,0,2:T(8,128)(2,1)} %bitcast.15) | data formatting | bytes 8388608 | tf_op jit(solution)/shard_map/all_to_all | solution.py:104
  443.0 1.3 copy.47
  (32 shorter events, 7.0 us)
Async XLA Ops:
  7.2 161.4 %all-gather.3.cloned.1.call-start = ((), (), s32[]{:S(2)}) async-start(), calls=%async_computation.5 | async-start | bytes 17825792 | tf_op jit(solution)/shard_map/all_gather | solution.py:86
  7.9 213.3 %reduce-scatter.3.cloned.1.call-start = ((), (), s32[]{:S(2)}) async-start(), calls=%async_computation.6 | async-start | bytes 2359296 | tf_op jit(solution)/shard_map/reduce_scatter | solution.py:22
  177.6 43.7 %copy-start = (f32[512,128]{1,0:T(8,128)S(1)}, f32[512,128]{1,0:T(8,128)}, u32[]{:S(2)}) copy-start(f32[512,128]{1,0:T(8,128)} %param.10) | copy-start | bytes 786436
  177.6 43.8 %copy-start.1 = (f32[512,128]{1,0:T(8,128)S(1)}, f32[512,128]{1,0:T(8,128)}, u32[]{:S(2)}) copy-start(f32[512,128]{1,0:T(8,128)} %param.11) | copy-start | bytes 786436
  177.6 43.9 %copy-start.2 = (f32[512,128]{1,0:T(8,128)S(1)}, f32[512,128]{1,0:T(8,128)}, u32[]{:S(2)}) copy-start(f32[512,128]{1,0:T(8,128)} %param.9) | copy-start | bytes 786436
  180.1 59.6 %reduce-scatter.5.cloned.1.call-start = ((), (), s32[]{:S(2)}) async-start(), calls=%async_computation.7 | async-start | bytes 393216 | tf_op jit(solution)/shard_map/reduce_scatter | solution.py:22
  221.2 83.7 %all-gather.5.cloned.1.call-start = ((), (), s32[]{:S(2)}) async-start(), calls=%async_computation.8 | async-start | bytes 2228224 | tf_op jit(solution)/shard_map/all_gather | solution.py:95
  244.3 85.2 %all-to-all-start.1 = ((bf16[16,512,128]{2,1,0:T(8,128)(2,1)}), bf16[16,512,128]{2,1,0:T(8,128)(2,1)S(1)}, u32[]{:S(2)}, u32[]{:S(2)}) async-start(bf16[16,512,128]{2,1,0:T(8,128)(2,1)} %broadcast_in_dim.78), calls=%async_computation.3 | async-start | bytes 4194304 | tf_op jit(solution)/shard_map/all_to_all | solution.py:38
  329.5 107.1 %all-to-all-start.2 = ((bf16[512,16,256]{0,2,1:T(8,128)(2,1)}), bf16[512,16,256]{0,2,1:T(8,128)(2,1)}, u32[]{:S(2)}, u32[]{:S(2)}) async-start(bf16[512,16,256]{0,2,1:T(8,128)(2,1)} %select_select_fusion), calls=%async_computation.4 | async-start | bytes 8388608 | tf_op jit(solution)/shard_map/all_to_all | solution.py:104
Sparse Core Ops, SparseCore 0:
  10.5 158.0 all-gather.2
  180.3 40.8 reduce-scatter.2
  223.7 16.0 reduce-scatter.4
  242.8 62.0 all-gather.4
where the time goes:
time: 452 us; the launch traced here: 451 us
  waiting for transfers between devices  270 us (60%)
  blocking collectives  73.9 us (16%)
  local copies, waits for them, and re-layouts  46.9 us (10%)
  other arithmetic  19.1 us (4%)
  starting transfers between devices  18.9 us (4%)
  between operations  13.9 us (3%)
  matrix products  8.12 us (2%)
    all_to_all x1, waiting for transfers between devices, on_device(): lax.all_to_all(outgoing, REP, split_axis=1, concat_axis=0, tiled=True)  93.3 us
    all_to_all x1, blocking collectives, on_device(): lax.all_to_all(spread, 'tp', split_axis=1, concat_axis=1, tiled=True)  73.9 us
    all_gather x1, waiting for transfers between devices, on_device(): lax.all_gather(tokens, 'tp', axis=1, tiled=True)  63.9 us
    reduce_scatter x2, waiting for transfers between devices, own_block(): parts = lax.psum_scatter(parts, axes[k], scatter_dimension=0, tiled=True)  59 us
    all_gather x1, waiting for transfers between devices, on_device(): replica_rows = lax.all_gather(weights, 'tp', axis=1, tiled=True)  52.9 us
    gather x1, local copies, waits for them, and re-layouts, on_device(): jnp.take(replica_rows, jnp.clip(source_cols, 0, COLS - 1).reshape(-1), ax...  19.3 us
    all_to_all x1, starting transfers between devices, on_device(): lax.all_to_all(outgoing, REP, split_axis=1, concat_axis=0, tiled=True)  11.3 us
    gather x1, local copies, waits for them, and re-layouts, on_device(): picked = jnp.take(grad_out, jnp.clip(offset, 0, slot_width - 1), axis=1)  9.61 us
  transfers between devices with their start and end apart: 6, of which 5 were waited for; matrix products, arithmetic and copies ran while one was open for 12% of the time, Pallas kernels for 0%

commit v1 on v0

--- a/solution.py
+++ b/solution.py
@@ -92,7 +92,7 @@
     new_master, new_first, new_second = adam_update(master, first, second, summed)
     weights = new_master.astype(jnp.bfloat16)
     healthy = gathered_copies(weights, REP, 0)
-    replica_rows = lax.all_gather(weights, "tp", axis=1, tiled=True)
+    replica_rows = jnp.concatenate(lax.all_gather(weights, "tp"), axis=1)
     slot_begins = jnp.sum(jnp.where(is_mine[None, :], begins_all, 0), axis=1)
     slot_lengths = jnp.sum(jnp.where(is_mine[None, :], lengths, 0), axis=1)
     within = jnp.arange(slot_width, dtype=jnp.int32)

time: 452 us -> 455 us (level)
  transfers between devices with their start and end apart: 6 -> 6, of which waited for: 5 -> 5; matrix products, arithmetic and copies ran while one was open for 12% -> 11% of each run, Pallas kernels for 0% -> 0%
where the time goes in v1:
time: 455 us; the launch traced here: 454 us
  waiting for transfers between devices  273 us (60%)
  blocking collectives  73.9 us (16%)
  local copies, waits for them, and re-layouts  47 us (10%)
  other arithmetic  19.3 us (4%)
  starting transfers between devices  18.9 us (4%)
  between operations  13.9 us (3%)
  matrix products  8.12 us (2%)
    all_to_all x1, waiting for transfers between devices, on_device(): lax.all_to_all(outgoing, REP, split_axis=1, concat_axis=0, tiled=True)  95.9 us
    all_to_all x1, blocking collectives, on_device(): lax.all_to_all(spread, 'tp', split_axis=1, concat_axis=1, tiled=True)  73.9 us
    all_gather x1, waiting for transfers between devices, on_device(): lax.all_gather(tokens, 'tp', axis=1, tiled=True)  63.9 us
    reduce_scatter x2, waiting for transfers between devices, own_block(): parts = lax.psum_scatter(parts, axes[k], scatter_dimension=0, tiled=True)  59.5 us
    all_gather x1, waiting for transfers between devices, on_device(): replica_rows = jnp.concatenate(lax.all_gather(weights, 'tp'), axis=1)  52.9 us
    gather x1, local copies, waits for them, and re-layouts, on_device(): jnp.take(replica_rows, jnp.clip(source_cols, 0, COLS - 1).reshape(-1), ax...  17.3 us
    all_to_all x1, starting transfers between devices, on_device(): lax.all_to_all(outgoing, REP, split_axis=1, concat_axis=0, tiled=True)  11.3 us
    gather x1, local copies, waits for them, and re-layouts, on_device(): picked = jnp.take(grad_out, jnp.clip(offset, 0, slot_width - 1), axis=1)  9.61 us
  transfers between devices with their start and end apart: 6, of which 5 were waited for; matrix products, arithmetic and copies ran while one was open for 11% of the time, Pallas kernels for 0%

profile of v1, /device:TPU:32, one launch (start us, length us, event | category | flops | bytes accessed | tf_op | source)
XLA Modules:
  0.0 454.0 jit_solution(642402272988602176)
XLA Ops:
  8.0 0.9 reduce_window_sum.11
  8.8 1.2 copy.19
  10.9 1.3 fusion.12
  12.9 9.6 %gather_fusion = bf16[2048,1024]{1,0:T(8,128)(2,1)} fusion(bf16[1024,256]{0,1:T(8,128)(2,1)S(1)} %copy.19, s32[2048]{0:T(1024)S(1)} %broadcast_clamp_fusion.1), kind=kCustom, calls=%fused_computation | custom fusion | bytes 8396800 | tf_op jit(solution)/shard_map/jit(_take)/gather | solution.py:79
  23.2 1.3 fusion.11
  24.5 3.1 select_select_fusion.1
  27.6 73.9 %all_to_all.25 = bf16[1024,16,128]{0,2,1:T(8,128)(2,1)} all-to-all(bf16[1024,16,128]{0,2,1:T(8,128)(2,1)S(1)} %select_select_fusion.1), channel_id=1, replica_groups=mesh['rep_0'=2,'rep_1'=8,'tp'=16] {'tp'}, dimensions={1} | all-to-all | bytes 8388608 | tf_op jit(solution)/shard_map/all_to_all | solution.py:83
  101.5 3.1 reduce_sum.50
  104.7 63.9 %all-gather.4.cloned.1.call-done = bf16[1024,8192]{1,0:T(8,128)(2,1)} async-done(((bf16[1024,512]{1,0:T(8,128)(2,1)}), bf16[1024,8192]{1,0:T(8,128)(2,1)}) %all-gather.4.cloned.1.call-update) | async-done | bytes 16777232 | tf_op jit(solution)/shard_map/all_gather | solution.py:86
  168.6 8.1 %convolution_convert_fusion = bf16[128,8192]{1,0:T(8,128)(2,1)S(1)} fusion(bf16[1024,128]{0,1:T(8,128)(2,1)S(1)} %reduce_sum.50, bf16[1024,8192]{1,0:T(8,128)(2,1)} %all-gather.4.cloned.1.call-done), kind=kOutput, calls=%fused_computation.2 | convolution fusion | flops 2148532224 | bytes 19136512 | tf_op jit(solution)/shard_map/dot_general | solution.py:85
  177.6 3.0 copy.20
  180.7 41.0 %reduce-scatter.3.cloned.1.call-done = bf16[2,512,128]{2,1,0:T(8,128)(2,1)} async-done(((bf16[16,512,128]{2,1,0:T(8,128)(2,1)}), bf16[2,512,128]{2,1,0:T(8,128)(2,1)}) %reduce-scatter.3.cloned.1.call-update) | async-done | bytes 262160 | tf_op jit(solution)/shard_map/reduce_scatter | solution.py:22
  221.8 18.5 %reduce-scatter.5.cloned.1.call-done = bf16[1,512,128]{2,1,0:T(8,128)(2,1)} async-done(((bf16[2,512,128]{2,1,0:T(8,128)(2,1)}), bf16[1,512,128]{2,1,0:T(8,128)(2,1)}) %reduce-scatter.5.cloned.1.call-update) | async-done | bytes 131088 | tf_op jit(solution)/shard_map/reduce_scatter | solution.py:22
  240.3 1.9 fusion.14
  242.2 2.6 broadcast_in_dim.78
  244.9 7.5 %all-to-all-start.1 = ((bf16[16,512,128]{2,1,0:T(8,128)(2,1)}), bf16[16,512,128]{2,1,0:T(8,128)(2,1)}, u32[]{:S(2)}, u32[]{:S(2)}) async-start(bf16[16,512,128]{2,1,0:T(8,128)(2,1)} %broadcast_in_dim.78), calls=%async_computation.3 | async-start | bytes 4194304 | tf_op jit(solution)/shard_map/all_to_all | solution.py:38
  252.6 52.9 %all-gather.6.cloned.1.call-done = bf16[8192,128]{1,0:T(8,128)(2,1)} async-done(((bf16[512,128]{1,0:T(8,128)(2,1)}), bf16[8192,128]{1,0:T(8,128)(2,1)}) %all-gather.6.cloned.1.call-update) | async-done | bytes 2097168 | tf_op jit(solution)/shard_map/all_gather | solution.py:95
  305.5 2.9 copy.21
  308.4 17.3 %gather_fusion.1 = bf16[4096,512]{1,0:T(8,128)(2,1)} fusion(bf16[512,2048]{0,1:T(8,128)(2,1)S(1)} %bitcast.47, s32[4096]{0:T(1024)S(1)} %broadcast_clamp_fusion), kind=kCustom, calls=%fused_computation.1 | custom fusion | bytes 8404992 | tf_op jit(solution)/shard_map/jit(_take)/gather | solution.py:101
  325.7 5.2 %select_select_fusion = bf16[512,16,256]{0,2,1:T(8,128)(2,1)} fusion(bf16[512,16,256]{0,2,1:T(8,128)(2,1)} %bitcast.48, pred[16,256]{1,0:T(8,128)(4,1)S(1)} %get-tuple-element.15, pred[16,256]{1,0:T(8,128)(4,1)S(1)} %get-tuple-element.14), kind=kLoop, calls=%fused_computation.3 | loop fusion | flops 4194304 | bytes 8396800 | tf_op jit(solution)/shard_map/jit(_where)/select_n | solution.py:102
  331.0 11.3 %all-to-all-start.2 = ((bf16[512,16,256]{0,2,1:T(8,128)(2,1)}), bf16[512,16,256]{0,2,1:T(8,128)(2,1)}, u32[]{:S(2)}, u32[]{:S(2)}) async-start(bf16[512,16,256]{0,2,1:T(8,128)(2,1)} %select_select_fusion), calls=%async_computation.4 | async-start | bytes 8388608 | tf_op jit(solution)/shard_map/all_to_all | solution.py:104
  342.2 95.9 %all-to-all-done.2 = bf16[512,16,256]{0,2,1:T(8,128)(2,1)} async-done(((bf16[512,16,256]{0,2,1:T(8,128)(2,1)}), bf16[512,16,256]{0,2,1:T(8,128)(2,1)}, u32[]{:S(2)}, u32[]{:S(2)}) %all-to-all-start.2) | async-done | bytes 4194336 | tf_op jit(solution)/shard_map/all_to_all | solution.py:104
  438.1 6.4 %copy.22 = bf16[16,512,1,256]{3,1,0,2:T(8,128)(2,1)} copy(bf16[16,512,1,256]{1,3,0,2:T(8,128)(2,1)} %bitcast.18) | data formatting | bytes 8388608 | tf_op jit(solution)/shard_map/all_to_all | solution.py:104
  444.5 3.0 copy.26
  (26 shorter events, 4.1 us)
Async XLA Ops:
  7.2 161.4 %all-gather.4.cloned.1.call-start = ((), (), s32[]{:S(2)}) async-start(), calls=%async_computation.5 | async-start | bytes 17825792 | tf_op jit(solution)/shard_map/all_gather | solution.py:86
  7.9 213.8 %reduce-scatter.3.cloned.1.call-start = ((), (), s32[]{:S(2)}) async-start(), calls=%async_computation.6 | async-start | bytes 2359296 | tf_op jit(solution)/shard_map/reduce_scatter | solution.py:22
  177.6 62.7 %copy-start = (f32[512,128]{1,0:T(8,128)S(1)}, f32[512,128]{1,0:T(8,128)}, u32[]{:S(2)}) copy-start(f32[512,128]{1,0:T(8,128)} %param.9) | copy-start | bytes 786436
  177.6 62.7 %copy-start.1 = (f32[512,128]{1,0:T(8,128)S(1)}, f32[512,128]{1,0:T(8,128)}, u32[]{:S(2)}) copy-start(f32[512,128]{1,0:T(8,128)} %param.11) | copy-start | bytes 786436
  177.6 62.7 %copy-start.2 = (f32[512,128]{1,0:T(8,128)S(1)}, f32[512,128]{1,0:T(8,128)}, u32[]{:S(2)}) copy-start(f32[512,128]{1,0:T(8,128)} %param.10) | copy-start | bytes 786436
  180.7 59.6 %reduce-scatter.5.cloned.1.call-start = ((), (), s32[]{:S(2)}) async-start(), calls=%async_computation.7 | async-start | bytes 393216 | tf_op jit(solution)/shard_map/reduce_scatter | solution.py:22
  221.7 83.8 %all-gather.6.cloned.1.call-start = ((), (), s32[]{:S(2)}) async-start(), calls=%async_computation.8 | async-start | bytes 2228224 | tf_op jit(solution)/shard_map/all_gather | solution.py:95
  244.9 86.1 %all-to-all-start.1 = ((bf16[16,512,128]{2,1,0:T(8,128)(2,1)}), bf16[16,512,128]{2,1,0:T(8,128)(2,1)}, u32[]{:S(2)}, u32[]{:S(2)}) async-start(bf16[16,512,128]{2,1,0:T(8,128)(2,1)} %broadcast_in_dim.78), calls=%async_computation.3 | async-start | bytes 4194304 | tf_op jit(solution)/shard_map/all_to_all | solution.py:38
  331.0 107.1 %all-to-all-start.2 = ((bf16[512,16,256]{0,2,1:T(8,128)(2,1)}), bf16[512,16,256]{0,2,1:T(8,128)(2,1)}, u32[]{:S(2)}, u32[]{:S(2)}) async-start(bf16[512,16,256]{0,2,1:T(8,128)(2,1)} %select_select_fusion), calls=%async_computation.4 | async-start | bytes 8388608 | tf_op jit(solution)/shard_map/all_to_all | solution.py:104
Sparse Core Ops, SparseCore 0:
  10.5 158.0 all-gather.3
  180.8 40.8 reduce-scatter.2
  224.2 16.0 reduce-scatter.4
  243.4 62.0 all-gather.5
